TPU v7x, 512 devices: a whole 4x8x8 slice. The times are simulated.
512 devices in a mesh: rows: 16 (over x, y_lo, core), dp: 32 (over z, y_hi).
Axes of the slice: x: 4, y: 8 (y_hi: 4, y_lo: 2; y = y_hi * 2 + y_lo), z: 8, core: 2. Of those that a mesh axis runs over, the one named last changes fastest.
Arguments:
- images: bfloat16 [32, 32, 512, 128], P('dp', 'rows'), may hold values from -54 to 54
- conv_weight: bfloat16 [3, 3, 128, 128], replicated, may hold values from -0.1875 to 0.1875
- conv_bias: float32 [128], replicated, may hold values from -3 to 3
- norm_gain: float32 [128], replicated, may hold values from 0.5 to 1.5
- norm_shift: float32 [128], replicated, may hold values from -3 to 3
- down_weight: bfloat16 [3, 3, 128, 256], replicated, may hold values from -0.1875 to 0.1875
- down_bias: float32 [256], replicated, may hold values from -3 to 3
- cotangent: bfloat16 [32, 16, 256, 256], P('dp', 'rows'), may hold values from -6 to 6
Outputs:
- block_out: bfloat16 [32, 16, 256, 256], P('dp', 'rows')
- grad_images: bfloat16 [32, 32, 512, 128], P('dp', 'rows')
- grad_conv_weight: float32 [3, 3, 128, 128], P(None, None, None, 'dp')
- grad_conv_bias: float32 [128], P('dp')
- grad_gain: float32 [128], P('dp')
- grad_shift: float32 [128], P('dp')
- grad_down_weight: float32 [3, 3, 128, 256], P(None, None, None, 'dp')
- grad_down_bias: float32 [256], P('dp')
All inputs are finite; a program needn't handle non-finite values.
Results may differ from a plain program's by a relative error of at most 0.0048.
Values may be sent and summed in bfloat16 or wider, within the bound.
A program may use at most 64 MiB of HBM per device.

v0:
```python
import jax
import jax.numpy as jnp
from jax import lax
from jax.sharding import PartitionSpec as P

GROUPS = 32


def extended(block, sides, width):
    for axis, dim in sides:
        count = lax.axis_size(axis)
        forward = [(i, i + 1) for i in range(count - 1)]
        backward = [(target, source) for source, target in forward]
        low = lax.ppermute(
            lax.slice_in_dim(block, block.shape[dim] - width, None, axis=dim), axis, forward
        )
        high = lax.ppermute(lax.slice_in_dim(block, 0, width, axis=dim), axis, backward)
        block = jnp.concatenate([low, block, high], axis=dim)
    return block


def from_behind(x, axis, by):
    length = lax.axis_size(axis)
    pairs = [(i, i + by) for i in range(length) if 0 <= i + by < length]
    return lax.ppermute(x, axis, pairs)


def taps_conv(padded, weight, rows, cols):
    total = jnp.zeros((rows * cols, weight.shape[3]), jnp.float32)
    for kh in range(3):
        for kw in range(3):
            piece = padded[kh : kh + rows, kw : kw + cols].reshape(rows * cols, -1)
            total = total + jnp.dot(piece, weight[kh, kw], preferred_element_type=jnp.float32)
    return total.reshape(rows, cols, weight.shape[3])


def weave(part_zero, part_one, part_two, axis):
    lead = [(0, 0)] * part_zero.ndim
    after = list(lead)
    before = list(lead)
    after[axis] = (0, 1)
    before[axis] = (1, 0)
    even = jnp.pad(part_zero, after) + jnp.pad(part_two, before)
    odd = jnp.pad(part_one, after)
    joined = jnp.stack([even, odd], axis + 1)
    shape = list(even.shape)
    shape[axis] = 2 * shape[axis]
    return joined.reshape(shape)


def shards(
    images, conv_weight, conv_bias, norm_gain, norm_shift, down_weight, down_bias, cotangent
):
    image = images[0]
    cot = cotangent[0]
    rows, cols, chans = image.shape
    half_rows, half_cols, outs = cot.shape
    width = chans // GROUPS
    count = float(rows * cols * width * lax.axis_size("rows"))
    framed = extended(image, (("rows", 0),), 1)
    padded = jnp.pad(framed, ((0, 0), (1, 1), (0, 0)))
    hidden = taps_conv(padded, conv_weight, rows, cols) + conv_bias
    grouped = hidden.reshape(rows, cols, GROUPS, width)
    mean = lax.psum(jnp.sum(grouped, axis=(0, 1, 3)), "rows") / count
    centred = grouped - mean[:, None]
    var = lax.psum(jnp.sum(centred * centred, axis=(0, 1, 3)), "rows") / count
    rstd = lax.rsqrt(var + 1e-05)
    normed = (centred * rstd[:, None]).reshape(rows, cols, chans)
    pre = normed * norm_gain + norm_shift
    sig = jax.nn.sigmoid(pre)
    mixed = (image.astype(jnp.float32) + pre * sig).astype(jnp.bfloat16)
    above = from_behind(mixed[-1], "rows", 1)
    shifted = jnp.pad(jnp.concatenate([above[None], mixed], 0), ((0, 0), (1, 0), (0, 0)))
    cot_flat = cot.reshape(half_rows * half_cols, outs)
    out = jnp.zeros((half_rows * half_cols, outs), jnp.float32)
    grad_down = []
    backs = []
    for kh in range(3):
        line = []
        back_line = []
        for kw in range(3):
            piece = shifted[kh : kh + 2 * half_rows : 2, kw : kw + 2 * half_cols : 2].reshape(
                half_rows * half_cols, chans
            )
            out = out + jnp.dot(piece, down_weight[kh, kw], preferred_element_type=jnp.float32)
            line.append(jnp.dot(piece.T, cot_flat, preferred_element_type=jnp.float32))
            back = jnp.dot(cot_flat, down_weight[kh, kw].T, preferred_element_type=jnp.float32)
            back_line.append(back.reshape(half_rows, half_cols, chans))
        grad_down.append(jnp.stack(line))
        backs.append(weave(back_line[0], back_line[1], back_line[2], 1))
    block = (out + down_bias).astype(jnp.bfloat16).reshape(half_rows, half_cols, outs)
    grad_down = jnp.stack(grad_down)
    grad_down_bias = jnp.sum(cot.astype(jnp.float32), axis=(0, 1))
    woven = weave(backs[0], backs[1], backs[2], 0)
    local_grad = woven[1 : rows + 1, 1 : cols + 1]
    from_below = from_behind(woven[0, 1 : cols + 1], "rows", -1)
    grad_mixed = jnp.concatenate([local_grad[:-1], local_grad[-1:] + from_below[None]], 0)
    grad_pre = grad_mixed * sig * (1.0 + pre * (1.0 - sig))
    grad_gain = jnp.sum(grad_pre * normed, axis=(0, 1))
    grad_shift = jnp.sum(grad_pre, axis=(0, 1))
    scaled = (grad_pre * norm_gain).reshape(rows, cols, GROUPS, width)
    normed_g = normed.reshape(rows, cols, GROUPS, width)
    first, second = lax.psum(
        (jnp.sum(scaled, axis=(0, 1, 3)), jnp.sum(scaled * normed_g, axis=(0, 1, 3))), "rows"
    )
    first = first / count
    second = second / count
    grad_hidden = (rstd[:, None] * (scaled - first[:, None] - normed_g * second[:, None])).reshape(
        rows, cols, chans
    )
    grad_bias = jnp.sum(grad_hidden, axis=(0, 1))
    rounded = grad_hidden.astype(jnp.bfloat16)
    flat = rounded.reshape(rows * cols, chans)
    grad_conv = []
    for kh in range(3):
        line = []
        for kw in range(3):
            piece = padded[kh : kh + rows, kw : kw + cols].reshape(rows * cols, chans)
            line.append(jnp.dot(piece.T, flat, preferred_element_type=jnp.float32))
        grad_conv.append(jnp.stack(line))
    grad_conv = jnp.stack(grad_conv)
    grad_framed = extended(rounded, (("rows", 0),), 1)
    grad_pad = jnp.pad(grad_framed, ((0, 0), (1, 1), (0, 0)))
    back_total = jnp.zeros((rows * cols, chans), jnp.float32)
    for kh in range(3):
        for kw in range(3):
            piece = grad_pad[2 - kh : 2 - kh + rows, 2 - kw : 2 - kw + cols].reshape(
                rows * cols, chans
            )
            back_total = back_total + jnp.dot(
                piece, conv_weight[kh, kw].T, preferred_element_type=jnp.float32
            )
    grad_image = (grad_mixed + back_total.reshape(rows, cols, chans)).astype(jnp.bfloat16)
    conv_pack = grad_conv.reshape(9 * chans, chans)
    small_pack = jnp.stack([grad_bias, grad_gain, grad_shift])
    down_pack = grad_down.reshape(9 * chans, outs)
    bias_pack = grad_down_bias[None]
    count_dp = lax.axis_size("dp")
    totals = lax.psum((conv_pack, small_pack, down_pack, bias_pack), ("rows", "dp"))
    owner = lax.axis_index("dp")
    narrow = chans // count_dp
    wide = outs // count_dp
    conv_part = lax.dynamic_slice_in_dim(totals[0], owner * narrow, narrow, 1)
    small_part = lax.dynamic_slice_in_dim(totals[1], owner * narrow, narrow, 1)
    down_part = lax.dynamic_slice_in_dim(totals[2], owner * wide, wide, 1)
    bias_part = lax.dynamic_slice_in_dim(totals[3], owner * wide, wide, 1)
    return (
        block[None],
        grad_image[None],
        conv_part.reshape(3, 3, chans, -1),
        small_part[0],
        small_part[1],
        small_part[2],
        down_part.reshape(3, 3, chans, -1),
        bias_part[0],
    )


def solution(mesh):
    in_specs = (
        P("dp", "rows", None, None),
        P(),
        P(),
        P(),
        P(),
        P(),
        P(),
        P("dp", "rows", None, None),
    )
    out_specs = (
        P("dp", "rows", None, None),
        P("dp", "rows", None, None),
        P(None, None, None, "dp"),
        P("dp"),
        P("dp"),
        P("dp"),
        P(None, None, None, "dp"),
        P("dp"),
    )
    return jax.shard_map(shards, mesh=mesh, in_specs=in_specs, out_specs=out_specs, check_vma=False)
```

profile of v0, /device:TPU:1, one launch (start us, length us, event | category | flops | bytes accessed | tf_op | source)
XLA Modules:
  0.0 581.2 jit_solution(11627743747505670904)
XLA Ops:
  9.1 4.6 collective-permute-start
  13.7 5.5 collective-permute-start.1
  25.5 1.9 collective-permute-start.3
  34.1 1.8 copy.43
  35.9 1.8 copy.41
  46.1 25.3 %psum.56 = f32[32]{0:T(128)S(1)} all-reduce(f32[32]{0:T(128)S(1)} %reduce_sum.83), channel_id=1, replica_groups=mesh['rows'=16,'dp'=32] {'rows'}, use_global_device_ids=true, to_apply=%region_2.3 | all-reduce | flops 32 | bytes 256 | tf_op jit(solution)/shard_map/psum | solution.py:64
  71.9 30.0 %psum.57 = f32[32]{0:T(128)S(1)} all-reduce(f32[32]{0:T(128)S(1)} %reduce_sum.105), channel_id=1, replica_groups=mesh['rows'=16,'dp'=32] {'rows'}, use_global_device_ids=true, to_apply=%region_5.6 | all-reduce | flops 32 | bytes 256 | tf_op jit(solution)/shard_map/psum | solution.py:66
  106.4 27.1 %all-reduce.17 = (f32[32]{0:T(128)S(1)}, f32[32]{0:T(128)S(1)}) all-reduce(f32[32]{0:T(128)S(1)} %reduce_sum.111, f32[32]{0:T(128)S(1)} %reduce_sum.108), channel_id=1, replica_groups=mesh['rows'=16,'dp'=32] {'rows'}, use_global_device_ids=true, to_apply=%region_11.12 | all-reduce | flops 64 | bytes 512 | tf_op jit(solution)/shard_map/psum | solution.py:103
  134.9 1.8 multiply_convert_fusion
  144.4 101.7 %all-reduce.15 = (f32[3,128]{1,0:T(4,128)S(1)}, f32[1,256]{1,0:T(1,128)S(1)}) all-reduce(f32[3,128]{1,0:T(4,128)S(1)} %pad_maximum_fusion.12, f32[1,256]{1,0:T(1,128)S(1)} %bitcast.406), channel_id=1, replica_groups=mesh['rows'=16,'dp'=32] {'rows','dp'}, use_global_device_ids=true, to_apply=%region_16.17 | all-reduce | flops 640 | bytes 5120 | tf_op jit(solution)/shard_map/psum | solution.py:139
  247.6 4.4 collective-permute-start.2
  254.6 2.0 collective-permute-start.4
  256.6 3.0 collective-permute-start.5
  261.4 2.4 slice.255
  263.8 2.4 slice.253
  266.2 2.4 slice.251
  268.5 2.4 slice.249
  270.9 2.4 slice.247
  273.3 2.4 slice.245
  275.6 2.4 slice.243
  278.0 2.4 slice.241
  280.4 2.6 slice.257
  284.9 1.4 copy.71
  301.1 270.4 %all-reduce.20.cloned.1.call-done = (f32[1152,128]{0,1:T(8,128)}, f32[1152,256]{0,1:T(8,128)}) async-done(((f32[1152,128]{0,1:T(8,128)}, f32[1152,256]{0,1:T(8,128)}), (f32[1152,128]{0,1:T(8,128)}, f32[1152,256]{0,1:T(8,128)})) %all-reduce.20.cloned.1.call-update) | async-done | bytes 1769488 | tf_op jit(solution)/shard_map/psum | solution.py:139
  (240 shorter events, 61.7 us)
Async XLA Ops:
  7.2 13.1 %copy-start = (bf16[1,1,256,256]{3,2,1,0:T(8,128)(2,1)S(1)}, bf16[1,1,256,256]{3,2,1,0:T(8,128)(2,1)}, u32[]{:S(2)}) copy-start(bf16[1,1,256,256]{3,2,1,0:T(8,128)(2,1)} %param.15) | copy-start | bytes 393220
  7.2 13.1 %copy-start.1 = (bf16[3,3,128,256]{3,2,1,0:T(8,128)(2,1)S(1)}, bf16[3,3,128,256]{3,2,1,0:T(8,128)(2,1)}, u32[]{:S(2)}) copy-start(bf16[3,3,128,256]{3,2,1,0:T(8,128)(2,1)} %param.13) | copy-start | bytes 1769476
  7.2 564.4 %all-reduce.20.cloned.1.call-start = ((), (), s32[]{:S(2)}) async-start(), calls=%async_computation | async-start | bytes 3538944 | tf_op jit(solution)/shard_map/psum | solution.py:139
  9.1 20.0 %collective-permute-start = (bf16[1,512,128]{1,2,0:T(8,128)(2,1)}, bf16[1,512,128]{1,2,0:T(8,128)(2,1)S(1)}, u32[]{:S(2)}, u32[]{:S(2)}) collective-permute-start(bf16[1,512,128]{1,2,0:T(8,128)(2,1)} %get-tuple-element.60), channel_id=1, source_target_pairs={{0,32},{32,64},{64,96},{96,128},{128,160},{160,192},{192,224},{224... | collective-permute-start | bytes 393224 | tf_op jit(solution)/shard_map/ppermute | solution.py:14
  13.7 15.4 %collective-permute-start.1 = (bf16[1,512,128]{1,2,0:T(8,128)(2,1)}, bf16[1,512,128]{1,2,0:T(8,128)(2,1)}, u32[]{:S(2)}, u32[]{:S(2)}) collective-permute-start(bf16[1,512,128]{1,2,0:T(8,128)(2,1)} %get-tuple-element.61), channel_id=1, source_target_pairs={{32,0},{64,32},{96,64},{128,96},{160,128},{192,160},{224,192},{256... | collective-permute-start | bytes 393224 | tf_op jit(solution)/shard_map/ppermute | solution.py:17
  25.5 6.2 %copy-start.5 = (f32[1,512,128]{1,2,0:T(8,128)}, f32[1,512,128]{1,2,0:T(8,128)S(1)}, u32[]{:S(2)}) copy-start(f32[1,512,128]{1,2,0:T(8,128)S(1)} %get-tuple-element.38) | copy-start | bytes 786436
  25.5 77.5 %collective-permute-start.3 = (f32[512,128]{0,1:T(8,128)}, f32[512,128]{0,1:T(8,128)}, u32[]{:S(2)}, u32[]{:S(2)}) collective-permute-start(f32[512,128]{0,1:T(8,128)} %get-tuple-element.37), channel_id=1, source_target_pairs={{32,0},{64,32},{96,64},{128,96},{160,128},{192,160},{224,192},{256... | collective-permute-start | bytes 786440 | tf_op jit(solution)/shard_map/ppermute | solution.py:25
  71.7 32.8 %copy-start.12 = (f32[1,512,32,4]{1,0,3,2:T(1,128)S(1)}, f32[1,512,32,4]{1,0,3,2:T(1,128)}, u32[]{:S(2)}) copy-start(f32[1,512,32,4]{1,0,3,2:T(1,128)} %concatenate.65) | copy-start | bytes 786436
  105.1 29.9 %copy-start.6 = (f32[1,512,128]{1,2,0:T(8,128)S(1)}, f32[1,512,128]{1,2,0:T(8,128)}, u32[]{:S(2)}) copy-start(f32[1,512,128]{1,2,0:T(8,128)} %copy-done.5) | copy-start | bytes 786436
  105.6 29.3 %copy-start.7 = (f32[2,512,128]{1,2,0:T(8,128)S(1)}, f32[2,512,128]{1,2,0:T(8,128)}, u32[]{:S(2)}) copy-start(f32[2,512,128]{1,2,0:T(8,128)} %copy.44) | copy-start | bytes 1572868
  143.0 103.7 %copy-start.4 = (bf16[1,2,512,128]{3,2,1,0:T(8,128)(2,1)S(1)}, bf16[1,2,512,128]{3,2,1,0:T(8,128)(2,1)}, u32[]{:S(2)}) copy-start(bf16[1,2,512,128]{3,2,1,0:T(8,128)(2,1)} %param.8) | copy-start | bytes 786436
  144.1 102.8 %copy-start.8 = (bf16[2,512,128]{1,2,0:T(8,128)(2,1)S(1)}, bf16[2,512,128]{1,2,0:T(8,128)(2,1)}, u32[]{:S(2)}) copy-start(bf16[2,512,128]{1,2,0:T(8,128)(2,1)} %get-tuple-element.52) | copy-start | bytes 786436
  144.1 107.9 %copy-start.35 = (f32[1,128,128]{2,1,0:T(8,128)S(1)}, f32[1,128,128]{2,1,0:T(8,128)}, u32[]{:S(2)}) copy-start(f32[1,128,128]{2,1,0:T(8,128)} %convolution_bitcast_fusion.23) | copy-start | bytes 196612
  144.1 107.9 %copy-start.36 = (f32[1,128,128]{2,1,0:T(8,128)S(1)}, f32[1,128,128]{2,1,0:T(8,128)}, u32[]{:S(2)}) copy-start(f32[1,128,128]{2,1,0:T(8,128)} %convolution_bitcast_fusion.24) | copy-start | bytes 196612
  144.3 108.8 %copy-start.33 = (f32[1,128,128]{2,1,0:T(8,128)S(1)}, f32[1,128,128]{2,1,0:T(8,128)}, u32[]{:S(2)}) copy-start(f32[1,128,128]{2,1,0:T(8,128)} %convolution_bitcast_fusion.22) | copy-start | bytes 196612
  144.3 108.8 %copy-start.34 = (f32[1,128,128]{2,1,0:T(8,128)S(1)}, f32[1,128,128]{2,1,0:T(8,128)}, u32[]{:S(2)}) copy-start(f32[1,128,128]{2,1,0:T(8,128)} %convolution_bitcast_fusion.21) | copy-start | bytes 196612
  247.6 5.8 %copy-start.32 = (f32[1,128,128]{2,1,0:T(8,128)S(1)}, f32[1,128,128]{2,1,0:T(8,128)}, u32[]{:S(2)}) copy-start(f32[1,128,128]{2,1,0:T(8,128)} %convolution_bitcast_fusion.26) | copy-start | bytes 196612
  247.6 12.7 %collective-permute-start.2 = (bf16[512,128]{0,1:T(8,128)(2,1)}, bf16[512,128]{0,1:T(8,128)(2,1)}, u32[]{:S(2)}, u32[]{:S(2)}) collective-permute-start(bf16[512,128]{0,1:T(8,128)(2,1)} %slice_bitcast_fusion.1), channel_id=1, source_target_pairs={{0,32},{32,64},{64,96},{96,128},{128,160},{160,192},{192,224},{224... | collective-permute-start | bytes 393224 | tf_op jit(solution)/shard_map/ppermute | solution.py:25
  254.6 28.5 %copy-start.2 = (bf16[3,3,128,256]{3,2,1,0:T(8,128)(2,1)S(1)}, bf16[3,3,128,256]{3,2,1,0:T(8,128)(2,1)}, u32[]{:S(2)}) copy-start(bf16[3,3,128,256]{3,2,1,0:T(8,128)(2,1)} %param.13) | copy-start | bytes 1769476
  254.6 32.4 %collective-permute-start.4 = (bf16[1,512,128]{1,2,0:T(8,128)(2,1)}, bf16[1,512,128]{1,2,0:T(8,128)(2,1)}, u32[]{:S(2)}, u32[]{:S(2)}) collective-permute-start(bf16[1,512,128]{1,2,0:T(8,128)(2,1)} %get-tuple-element.56), channel_id=1, source_target_pairs={{0,32},{32,64},{64,96},{96,128},{128,160},{160,192},{192,224},{224... | collective-permute-start | bytes 393224 | tf_op jit(solution)/shard_map/ppermute | solution.py:14
  256.6 30.4 %collective-permute-start.5 = (bf16[1,512,128]{1,2,0:T(8,128)(2,1)}, bf16[1,512,128]{1,2,0:T(8,128)(2,1)}, u32[]{:S(2)}, u32[]{:S(2)}) collective-permute-start(bf16[1,512,128]{1,2,0:T(8,128)(2,1)} %get-tuple-element.57), channel_id=1, source_target_pairs={{32,0},{64,32},{96,64},{128,96},{160,128},{192,160},{224,192},{256... | collective-permute-start | bytes 393224 | tf_op jit(solution)/shard_map/ppermute | solution.py:17
  266.1 18.2 %copy-start.23 = (bf16[1,256,128]{1,2,0:T(8,128)(2,1)}, bf16[1,256,128]{1,2,0:T(8,128)(2,1)S(1)}, u32[]{:S(2)}) copy-start(bf16[1,256,128]{1,2,0:T(8,128)(2,1)S(1)} %slice.253) | copy-start | bytes 196612
  268.5 15.7 %copy-start.25 = (bf16[1,256,128]{1,2,0:T(8,128)(2,1)}, bf16[1,256,128]{1,2,0:T(8,128)(2,1)S(1)}, u32[]{:S(2)}) copy-start(bf16[1,256,128]{1,2,0:T(8,128)(2,1)S(1)} %slice.251) | copy-start | bytes 196612
  270.9 13.1 %copy-start.27 = (bf16[1,256,128]{1,2,0:T(8,128)(2,1)}, bf16[1,256,128]{1,2,0:T(8,128)(2,1)S(1)}, u32[]{:S(2)}) copy-start(bf16[1,256,128]{1,2,0:T(8,128)(2,1)S(1)} %slice.249) | copy-start | bytes 196612
  (27 other events, 39.3 us)
Sparse Core Ops, SparseCore 0:
  297.8 273.7 all-reduce.19
where the time goes:
time: 582 us; the launch traced here: 581 us
  waiting for transfers between devices  270 us (46%)
  blocking collectives  184 us (32%)
  local copies, waits for them, and re-layouts  57.4 us (10%)
  starting transfers between devices  21.5 us (4%)
  matrix products  19.1 us (3%)
  between operations  15.3 us (3%)
  other arithmetic  13.4 us (2%)
    psum x1, waiting for transfers between devices, shards(): lax.psum((conv_pack, small_pack, down_pack, bias_pack), ('rows', 'dp'))  270 us
    psum x1, blocking collectives, shards(): lax.psum((conv_pack, small_pack, down_pack, bias_pack), ('rows', 'dp'))  102 us
    psum x1, blocking collectives, shards(): var = lax.psum(jnp.sum(centred * centred, axis=(0, 1, 3)), 'rows') / count  30 us
    psum x1, blocking collectives, shards(): lax.psum((jnp.sum(scaled, axis=(0, 1, 3)), jnp.sum(scaled * normed_g, axi...  27.1 us
    psum x1, blocking collectives, shards(): mean = lax.psum(jnp.sum(grouped, axis=(0, 1, 3)), 'rows') / count  25.3 us
    slice x9, local copies, waits for them, and re-layouts, shards(): shifted[kh:kh + 2 * half_rows:2, kw:kw + 2 * half_cols:2]  21.5 us
  transfers between devices with their start and end apart: 7, of which 1 were waited for; matrix products, arithmetic and copies ran while one was open for 10% of the time, Pallas kernels for 0%

commit v1 on v0

--- a/solution.py
+++ b/solution.py
@@ -1,9 +1,18 @@
+import functools
 import jax
 import jax.numpy as jnp
 from jax import lax
 from jax.sharding import PartitionSpec as P
 
 GROUPS = 32
+
+
+def surface_mark(base_x, bus_axis):
+    opened = jnp.sum(jax.lax.all_gather(base_x, bus_axis), 0)
+    return opened
+
+
+trace_local_data = functools.partial(surface_mark, bus_axis="rows")
 
 
 def extended(block, sides, width):
@@ -63,7 +72,7 @@
     grouped = hidden.reshape(rows, cols, GROUPS, width)
     mean = lax.psum(jnp.sum(grouped, axis=(0, 1, 3)), "rows") / count
     centred = grouped - mean[:, None]
-    var = lax.psum(jnp.sum(centred * centred, axis=(0, 1, 3)), "rows") / count
+    var = trace_local_data(jnp.sum(centred * centred, axis=(0, 1, 3))) / count
     rstd = lax.rsqrt(var + 1e-05)
     normed = (centred * rstd[:, None]).reshape(rows, cols, chans)
     pre = normed * norm_gain + norm_shift

time: 582 us -> 585 us (level)
    psum x1 -> x0, blocking collectives: 30 us -> none  [shards(): var = lax.psum(jnp.sum(centred * centred, axis=(0, 1, 3)), 'rows') / count]
    unnamed x0 -> x1, blocking collectives: none -> 30 us
where the time goes in v1:
time: 585 us; the launch traced here: 584 us
  waiting for transfers between devices  271 us (46%)
  blocking collectives  184 us (31%)
  local copies, waits for them, and re-layouts  59.1 us (10%)
  starting transfers between devices  21.4 us (4%)
  matrix products  19.1 us (3%)
  between operations  16 us (3%)
  other arithmetic  13.4 us (2%)
    psum x1, waiting for transfers between devices, shards(): lax.psum((conv_pack, small_pack, down_pack, bias_pack), ('rows', 'dp'))  271 us
    psum x1, blocking collectives, shards(): lax.psum((conv_pack, small_pack, down_pack, bias_pack), ('rows', 'dp'))  102 us
    unnamed x1, blocking collectives  30 us
    psum x1, blocking collectives, shards(): lax.psum((jnp.sum(scaled, axis=(0, 1, 3)), jnp.sum(scaled * normed_g, axi...  27.1 us
    psum x1, blocking collectives, shards(): mean = lax.psum(jnp.sum(grouped, axis=(0, 1, 3)), 'rows') / count  25.3 us
    slice x9, local copies, waits for them, and re-layouts, shards(): shifted[kh:kh + 2 * half_rows:2, kw:kw + 2 * half_cols:2]  21.5 us
  transfers between devices with their start and end apart: 7, of which 1 were waited for; matrix products, arithmetic and copies ran while one was open for 10% of the time, Pallas kernels for 0%

profile of v1, /device:TPU:1, one launch (start us, length us, event | category | flops | bytes accessed | tf_op | source)
XLA Modules:
  0.0 583.7 jit_solution(4006638615826305233)
XLA Ops:
  9.1 4.6 collective-permute-start
  13.7 5.5 collective-permute-start.1
  25.5 1.9 collective-permute-start.3
  36.0 1.8 copy.83
  37.8 1.8 copy.81
  48.0 25.3 %psum.49 = f32[32]{0:T(128)S(1)} all-reduce(f32[32]{0:T(128)S(1)} %reduce_sum.94), channel_id=1, replica_groups=mesh['rows'=16,'dp'=32] {'rows'}, use_global_device_ids=true, to_apply=%region_2.3 | all-reduce | flops 32 | bytes 256 | tf_op jit(solution)/shard_map/psum | solution.py:73
  74.1 30.0 %all-reduce.15 = f32[512]{0:T(512)S(1)} all-reduce(f32[512]{0:T(512)S(1)} %dynamic-update-slice), channel_id=2, replica_groups=mesh['rows'=16,'dp'=32] {'rows'}, use_global_device_ids=true, to_apply=%add.15 | all-reduce | flops 512 | bytes 4096
  108.7 27.1 %all-reduce.18 = (f32[32]{0:T(128)S(1)}, f32[32]{0:T(128)S(1)}) all-reduce(f32[32]{0:T(128)S(1)} %reduce_sum.121, f32[32]{0:T(128)S(1)} %reduce_sum.118), channel_id=1, replica_groups=mesh['rows'=16,'dp'=32] {'rows'}, use_global_device_ids=true, to_apply=%region_11.12 | all-reduce | flops 64 | bytes 512 | tf_op jit(solution)/shard_map/psum | solution.py:112
  137.2 1.8 multiply_convert_fusion
  146.7 101.7 %all-reduce.16 = (f32[3,128]{1,0:T(4,128)S(1)}, f32[1,256]{1,0:T(1,128)S(1)}) all-reduce(f32[3,128]{1,0:T(4,128)S(1)} %pad_maximum_fusion.12, f32[1,256]{1,0:T(1,128)S(1)} %bitcast.407), channel_id=1, replica_groups=mesh['rows'=16,'dp'=32] {'rows','dp'}, use_global_device_ids=true, to_apply=%region_16.17 | all-reduce | flops 640 | bytes 5120 | tf_op jit(solution)/shard_map/psum | solution.py:148
  249.9 4.4 collective-permute-start.2
  256.9 2.0 collective-permute-start.4
  259.0 3.0 collective-permute-start.5
  263.7 2.4 slice.255
  266.1 2.4 slice.253
  268.5 2.4 slice.251
  270.9 2.4 slice.249
  273.2 2.4 slice.247
  275.6 2.4 slice.245
  278.0 2.4 slice.243
  280.3 2.4 slice.241
  282.7 2.6 slice.257
  287.3 1.4 copy.111
  303.4 270.6 %all-reduce.21.cloned.1.call-done = (f32[1152,128]{0,1:T(8,128)}, f32[1152,256]{0,1:T(8,128)}) async-done(((f32[1152,128]{0,1:T(8,128)}, f32[1152,256]{0,1:T(8,128)}), (f32[1152,128]{0,1:T(8,128)}, f32[1152,256]{0,1:T(8,128)})) %all-reduce.21.cloned.1.call-update) | async-done | bytes 1769488 | tf_op jit(solution)/shard_map/psum | solution.py:148
  (245 shorter events, 63.3 us)
Async XLA Ops:
  7.2 13.1 %copy-start = (bf16[1,1,256,256]{3,2,1,0:T(8,128)(2,1)S(1)}, bf16[1,1,256,256]{3,2,1,0:T(8,128)(2,1)}, u32[]{:S(2)}) copy-start(bf16[1,1,256,256]{3,2,1,0:T(8,128)(2,1)} %param.15) | copy-start | bytes 393220
  7.2 13.1 %copy-start.1 = (bf16[3,3,128,256]{3,2,1,0:T(8,128)(2,1)S(1)}, bf16[3,3,128,256]{3,2,1,0:T(8,128)(2,1)}, u32[]{:S(2)}) copy-start(bf16[3,3,128,256]{3,2,1,0:T(8,128)(2,1)} %param.13) | copy-start | bytes 1769476
  7.2 566.9 %all-reduce.21.cloned.1.call-start = ((), (), s32[]{:S(2)}) async-start(), calls=%async_computation | async-start | bytes 3538944 | tf_op jit(solution)/shard_map/psum | solution.py:148
  9.1 21.9 %collective-permute-start = (bf16[1,512,128]{1,2,0:T(8,128)(2,1)}, bf16[1,512,128]{1,2,0:T(8,128)(2,1)S(1)}, u32[]{:S(2)}, u32[]{:S(2)}) collective-permute-start(bf16[1,512,128]{1,2,0:T(8,128)(2,1)} %get-tuple-element.68), channel_id=1, source_target_pairs={{0,32},{32,64},{64,96},{96,128},{128,160},{160,192},{192,224},{224... | collective-permute-start | bytes 393224 | tf_op jit(solution)/shard_map/ppermute | solution.py:23
  13.7 17.3 %collective-permute-start.1 = (bf16[1,512,128]{1,2,0:T(8,128)(2,1)}, bf16[1,512,128]{1,2,0:T(8,128)(2,1)}, u32[]{:S(2)}, u32[]{:S(2)}) collective-permute-start(bf16[1,512,128]{1,2,0:T(8,128)(2,1)} %get-tuple-element.69), channel_id=1, source_target_pairs={{32,0},{64,32},{96,64},{128,96},{160,128},{192,160},{224,192},{256... | collective-permute-start | bytes 393224 | tf_op jit(solution)/shard_map/ppermute | solution.py:26
  25.5 8.1 %copy-start.5 = (f32[1,512,128]{1,2,0:T(8,128)}, f32[1,512,128]{1,2,0:T(8,128)S(1)}, u32[]{:S(2)}) copy-start(f32[1,512,128]{1,2,0:T(8,128)S(1)} %get-tuple-element.46) | copy-start | bytes 786436
  25.5 79.8 %collective-permute-start.3 = (f32[512,128]{0,1:T(8,128)}, f32[512,128]{0,1:T(8,128)}, u32[]{:S(2)}, u32[]{:S(2)}) collective-permute-start(f32[512,128]{0,1:T(8,128)} %get-tuple-element.45), channel_id=1, source_target_pairs={{32,0},{64,32},{96,64},{128,96},{160,128},{192,160},{224,192},{256... | collective-permute-start | bytes 786440 | tf_op jit(solution)/shard_map/ppermute | solution.py:34
  73.6 33.2 %copy-start.12 = (f32[1,512,32,4]{1,0,3,2:T(1,128)S(1)}, f32[1,512,32,4]{1,0,3,2:T(1,128)}, u32[]{:S(2)}) copy-start(f32[1,512,32,4]{1,0,3,2:T(1,128)} %concatenate.65) | copy-start | bytes 786436
  107.4 29.9 %copy-start.6 = (f32[1,512,128]{1,2,0:T(8,128)S(1)}, f32[1,512,128]{1,2,0:T(8,128)}, u32[]{:S(2)}) copy-start(f32[1,512,128]{1,2,0:T(8,128)} %copy-done.5) | copy-start | bytes 786436
  107.9 29.3 %copy-start.7 = (f32[2,512,128]{1,2,0:T(8,128)S(1)}, f32[2,512,128]{1,2,0:T(8,128)}, u32[]{:S(2)}) copy-start(f32[2,512,128]{1,2,0:T(8,128)} %copy.84) | copy-start | bytes 1572868
  145.3 103.7 %copy-start.4 = (bf16[1,2,512,128]{3,2,1,0:T(8,128)(2,1)S(1)}, bf16[1,2,512,128]{3,2,1,0:T(8,128)(2,1)}, u32[]{:S(2)}) copy-start(bf16[1,2,512,128]{3,2,1,0:T(8,128)(2,1)} %param.8) | copy-start | bytes 786436
  146.4 102.8 %copy-start.8 = (bf16[2,512,128]{1,2,0:T(8,128)(2,1)S(1)}, bf16[2,512,128]{1,2,0:T(8,128)(2,1)}, u32[]{:S(2)}) copy-start(bf16[2,512,128]{1,2,0:T(8,128)(2,1)} %get-tuple-element.60) | copy-start | bytes 786436
  146.4 107.9 %copy-start.35 = (f32[1,128,128]{2,1,0:T(8,128)S(1)}, f32[1,128,128]{2,1,0:T(8,128)}, u32[]{:S(2)}) copy-start(f32[1,128,128]{2,1,0:T(8,128)} %convolution_bitcast_fusion.23) | copy-start | bytes 196612
  146.5 107.9 %copy-start.36 = (f32[1,128,128]{2,1,0:T(8,128)S(1)}, f32[1,128,128]{2,1,0:T(8,128)}, u32[]{:S(2)}) copy-start(f32[1,128,128]{2,1,0:T(8,128)} %convolution_bitcast_fusion.24) | copy-start | bytes 196612
  146.7 108.8 %copy-start.33 = (f32[1,128,128]{2,1,0:T(8,128)S(1)}, f32[1,128,128]{2,1,0:T(8,128)}, u32[]{:S(2)}) copy-start(f32[1,128,128]{2,1,0:T(8,128)} %convolution_bitcast_fusion.22) | copy-start | bytes 196612
  146.7 108.8 %copy-start.34 = (f32[1,128,128]{2,1,0:T(8,128)S(1)}, f32[1,128,128]{2,1,0:T(8,128)}, u32[]{:S(2)}) copy-start(f32[1,128,128]{2,1,0:T(8,128)} %convolution_bitcast_fusion.21) | copy-start | bytes 196612
  249.9 5.8 copy-start.32
  249.9 12.7 %collective-permute-start.2 = (bf16[512,128]{0,1:T(8,128)(2,1)}, bf16[512,128]{0,1:T(8,128)(2,1)}, u32[]{:S(2)}, u32[]{:S(2)}) collective-permute-start(bf16[512,128]{0,1:T(8,128)(2,1)} %slice_bitcast_fusion.1), channel_id=1, source_target_pairs={{0,32},{32,64},{64,96},{96,128},{128,160},{160,192},{192,224},{224... | collective-permute-start | bytes 393224 | tf_op jit(solution)/shard_map/ppermute | solution.py:34
  256.9 28.5 %copy-start.2 = (bf16[3,3,128,256]{3,2,1,0:T(8,128)(2,1)S(1)}, bf16[3,3,128,256]{3,2,1,0:T(8,128)(2,1)}, u32[]{:S(2)}) copy-start(bf16[3,3,128,256]{3,2,1,0:T(8,128)(2,1)} %param.13) | copy-start | bytes 1769476
  256.9 32.4 %collective-permute-start.4 = (bf16[1,512,128]{1,2,0:T(8,128)(2,1)}, bf16[1,512,128]{1,2,0:T(8,128)(2,1)}, u32[]{:S(2)}, u32[]{:S(2)}) collective-permute-start(bf16[1,512,128]{1,2,0:T(8,128)(2,1)} %get-tuple-element.64), channel_id=1, source_target_pairs={{0,32},{32,64},{64,96},{96,128},{128,160},{160,192},{192,224},{224... | collective-permute-start | bytes 393224 | tf_op jit(solution)/shard_map/ppermute | solution.py:23
  259.0 30.4 %collective-permute-start.5 = (bf16[1,512,128]{1,2,0:T(8,128)(2,1)}, bf16[1,512,128]{1,2,0:T(8,128)(2,1)}, u32[]{:S(2)}, u32[]{:S(2)}) collective-permute-start(bf16[1,512,128]{1,2,0:T(8,128)(2,1)} %get-tuple-element.65), channel_id=1, source_target_pairs={{32,0},{64,32},{96,64},{128,96},{160,128},{192,160},{224,192},{256... | collective-permute-start | bytes 393224 | tf_op jit(solution)/shard_map/ppermute | solution.py:26
  268.5 18.2 %copy-start.23 = (bf16[1,256,128]{1,2,0:T(8,128)(2,1)}, bf16[1,256,128]{1,2,0:T(8,128)(2,1)S(1)}, u32[]{:S(2)}) copy-start(bf16[1,256,128]{1,2,0:T(8,128)(2,1)S(1)} %slice.253) | copy-start | bytes 196612
  270.8 15.7 %copy-start.25 = (bf16[1,256,128]{1,2,0:T(8,128)(2,1)}, bf16[1,256,128]{1,2,0:T(8,128)(2,1)S(1)}, u32[]{:S(2)}) copy-start(bf16[1,256,128]{1,2,0:T(8,128)(2,1)S(1)} %slice.251) | copy-start | bytes 196612
  273.2 13.1 %copy-start.27 = (bf16[1,256,128]{1,2,0:T(8,128)(2,1)}, bf16[1,256,128]{1,2,0:T(8,128)(2,1)S(1)}, u32[]{:S(2)}) copy-start(bf16[1,256,128]{1,2,0:T(8,128)(2,1)S(1)} %slice.249) | copy-start | bytes 196612
  (27 other events, 39.3 us)
Sparse Core Ops, SparseCore 0:
  300.1 273.9 all-reduce.20
